TPU v7x, 32 devices: a whole 2x2x4 slice. The times are simulated.
32 devices in a mesh: dp: 8 (over y, x, core), tensor: 4 (over z).
Axes of the slice: x: 2, y: 2, z: 4, core: 2. Of those that a mesh axis runs over, the one named last changes fastest.
Arguments:
- block_input: bfloat16 [4096, 1024], P('dp'), may hold values from -6 to 6
- cotangent: bfloat16 [4096, 1024], P('dp'), may hold values from -6 to 6
- seq_lengths: int32 [8, 4], P('dp'), may hold values from 0 to 512, as said below
- norm_gains: float32 [2, 2, 1024], replicated, may hold values from 0.1 to 1.9
- norm_biases: float32 [2, 2, 1024], replicated, may hold values from -3 to 3
- w_qkv: bfloat16 [2, 1024, 3, 1024], P(None, None, None, 'tensor'), may hold values from -0.1875 to 0.1875
- qv_bias: float32 [2, 2, 1024], P(None, None, 'tensor'), may hold values from -3 to 3
- w_out: bfloat16 [2, 1024, 1024], P(None, 'tensor'), may hold values from -0.375 to 0.375
- out_biases: float32 [2, 2, 1024], replicated, may hold values from -3 to 3
- w_up: bfloat16 [2, 1024, 4096], P(None, None, 'tensor'), may hold values from -0.1875 to 0.1875
- up_bias: float32 [2, 4096], P(None, 'tensor'), may hold values from -3 to 3
- w_down: bfloat16 [2, 4096, 1024], P(None, 'tensor'), may hold values from -0.09375 to 0.09375
Outputs:
- block_output: bfloat16 [4096, 1024], P('dp')
- input_grad: float32 [4096, 1024], P('dp')
- grad_norm_gains: float32 [2, 2, 1024], replicated
- grad_norm_biases: float32 [2, 2, 1024], replicated
- grad_w_qkv: float32 [2, 1024, 3, 1024], P(None, 'dp', None, 'tensor')
- grad_qv_bias: float32 [2, 2, 1024], P(None, None, 'tensor')
- grad_w_out: float32 [2, 1024, 1024], P(None, 'tensor', 'dp')
- grad_out_biases: float32 [2, 2, 1024], replicated
- grad_w_up: float32 [2, 1024, 4096], P(None, 'dp', 'tensor')
- grad_up_bias: float32 [2, 4096], P(None, 'tensor')
- grad_w_down: float32 [2, 4096, 1024], P(None, 'tensor', 'dp')
Inputs may be any that keep to these rules, and one draw needn't show every extreme that they name: `seq_lengths`: each row's lengths sum to at most 512; zero lengths occur; in every draw one row holds a single sequence of exactly 512 tokens.
All inputs are finite; a program needn't handle non-finite values.
Results may differ from a plain program's by a relative error of at most 0.025.
Values may be sent and summed in bfloat16 or wider, within the bound.
A program may use at most 128 MiB of HBM per device.

v0:
```python
import jax
import jax.numpy as jnp
from jax import lax
from jax.sharding import PartitionSpec as P

HEADS = 16
HEAD_DIM = 64


NORM_EPS = 1e-05


def layer_norm(residual, gain_vec, shift_vec):
    mean_row = jnp.mean(residual, axis=-1, keepdims=True)
    centered = residual - mean_row
    variance = jnp.mean(centered * centered, axis=-1, keepdims=True)
    return centered * lax.rsqrt(variance + NORM_EPS) * gain_vec + shift_vec


def gelu_tanh(pre_act):
    return (
        0.5
        * pre_act
        * (1.0 + jnp.tanh(0.7978845608028654 * (pre_act + 0.044715 * pre_act * pre_act * pre_act)))
    )


def norm_back(residual, gain_vec, shift_vec, grad_normed):
    result, pull_back = jax.vjp(layer_norm, residual, gain_vec, shift_vec)
    return pull_back(grad_normed)


def segment_mask(lengths, row_count):
    seq_ends = jnp.cumsum(lengths)
    position = jnp.arange(row_count, dtype=jnp.int32)
    segment = jnp.sum((position[:, None] >= seq_ends[None, :]).astype(jnp.int32), axis=1)
    same_seq = (segment[:, None] == segment[None, :]) & (position[None, :] <= position[:, None])
    row_gap = (position[:, None] - position[None, :]).astype(jnp.float32)
    live_rows = (position < seq_ends[-1]).astype(jnp.float32)
    return (same_seq, row_gap, live_rows)


def on_device(
    block_input,
    cotangent,
    seq_lengths,
    norm_gains,
    norm_biases,
    w_qkv,
    qv_bias,
    w_out,
    out_biases,
    w_up,
    up_bias,
    w_down,
):
    row_count = block_input.shape[0]
    my_rank = lax.axis_index("tensor")
    local_width = w_qkv.shape[3]
    heads_here = local_width // HEAD_DIM
    depth = w_qkv.shape[0]
    score_scale = HEAD_DIM ** (-0.5)
    f32 = jnp.float32
    same_seq, row_gap, live_rows = segment_mask(seq_lengths[0], row_count)
    head_index = my_rank * heads_here + jnp.arange(heads_here, dtype=jnp.int32) + 1
    slopes = jnp.exp2(-8.0 * head_index.astype(f32) / HEADS)

    def branch_total(partial_value):
        return lax.psum(partial_value.astype(jnp.bfloat16), "tensor").astype(jnp.float32)

    def input_total(partial_value):
        return lax.psum(partial_value.astype(jnp.bfloat16), "tensor").astype(jnp.float32)

    def score_block(queries, key_rows):
        raw_scores = (
            jnp.einsum("the,she->hts", queries, key_rows, preferred_element_type=f32) * score_scale
        )
        raw_scores = raw_scores - slopes[:, None, None] * row_gap
        return jnp.where(same_seq, raw_scores, -1000000000.0)

    head_shape = (row_count, heads_here, HEAD_DIM)
    residual = block_input.astype(f32)
    stored = []
    for layer_idx in range(depth):
        entering = residual
        normed = layer_norm(residual, norm_gains[layer_idx, 0], norm_biases[layer_idx, 0]).astype(
            jnp.bfloat16
        )
        projected = jnp.einsum("td,dcn->tcn", normed, w_qkv[layer_idx], preferred_element_type=f32)
        queries = (projected[:, 0] + qv_bias[layer_idx, 0]).astype(jnp.bfloat16).reshape(head_shape)
        key_rows = projected[:, 1].astype(jnp.bfloat16).reshape(head_shape)
        value_rows = (
            (projected[:, 2] + qv_bias[layer_idx, 1]).astype(jnp.bfloat16).reshape(head_shape)
        )
        scores = score_block(queries, key_rows)
        row_max = jnp.max(scores, axis=-1, keepdims=True)
        log_total = row_max + jnp.log(jnp.sum(jnp.exp(scores - row_max), axis=-1, keepdims=True))
        softmax_p = jnp.exp(scores - log_total).astype(jnp.bfloat16)
        context = jnp.einsum("hts,she->the", softmax_p, value_rows, preferred_element_type=f32)
        context = context.astype(jnp.bfloat16).reshape(row_count, local_width)
        partial_value = jnp.dot(context, w_out[layer_idx], preferred_element_type=f32)
        residual = residual + branch_total(partial_value) + out_biases[layer_idx, 0]
        middle = residual
        normed_mlp = layer_norm(
            residual, norm_gains[layer_idx, 1], norm_biases[layer_idx, 1]
        ).astype(jnp.bfloat16)
        up_proj = (
            jnp.dot(normed_mlp, w_up[layer_idx], preferred_element_type=f32) + up_bias[layer_idx]
        )
        activated = gelu_tanh(up_proj).astype(jnp.bfloat16)
        partial_value = jnp.dot(activated, w_down[layer_idx], preferred_element_type=f32)
        residual = residual + branch_total(partial_value) + out_biases[layer_idx, 1]
        stored.append(
            (
                entering,
                normed,
                queries,
                key_rows,
                value_rows,
                log_total,
                context,
                middle,
                normed_mlp,
                up_proj,
                activated,
            )
        )
    block_rows = residual.astype(jnp.bfloat16)
    grad_rows = cotangent.astype(f32) * live_rows[:, None]
    small_parts = []
    heavy_parts = []
    for layer_idx in reversed(range(depth)):
        (
            entering,
            normed,
            queries,
            key_rows,
            value_rows,
            log_total,
            context,
            middle,
            normed_mlp,
            up_proj,
            activated,
        ) = stored[layer_idx]
        down_bias_grad = jnp.sum(grad_rows, axis=0)
        grad_low = grad_rows.astype(jnp.bfloat16)
        down_w_grad = jnp.einsum("tf,td->fd", activated, grad_low, preferred_element_type=f32)
        act_grad = jnp.einsum("td,fd->tf", grad_low, w_down[layer_idx], preferred_element_type=f32)
        up_grad = jax.vjp(gelu_tanh, up_proj)[1](act_grad)[0].astype(jnp.bfloat16)
        up_bias_grad = jnp.sum(up_grad.astype(f32), axis=0)
        up_w_grad = jnp.einsum("td,tf->df", normed_mlp, up_grad, preferred_element_type=f32)
        normed_grad = input_total(
            jnp.einsum("tf,df->td", up_grad, w_up[layer_idx], preferred_element_type=f32)
        )
        middle_grad, gain_mlp, shift_mlp = norm_back(
            middle, norm_gains[layer_idx, 1], norm_biases[layer_idx, 1], normed_grad
        )
        grad_rows = grad_rows + middle_grad
        out_bias_grad = jnp.sum(grad_rows, axis=0)
        grad_low = grad_rows.astype(jnp.bfloat16)
        out_w_grad = jnp.einsum("tn,td->nd", context, grad_low, preferred_element_type=f32)
        context_grad = jnp.einsum(
            "td,nd->tn", grad_low, w_out[layer_idx], preferred_element_type=f32
        )
        context_grad = context_grad.astype(jnp.bfloat16).reshape(head_shape)
        scores = score_block(queries, key_rows)
        softmax_f = jnp.exp(scores - log_total)
        prob_grad = jnp.einsum("the,she->hts", context_grad, value_rows, preferred_element_type=f32)
        score_grad = softmax_f * (
            prob_grad - jnp.sum(prob_grad * softmax_f, axis=-1, keepdims=True)
        )
        score_grad = score_grad.astype(jnp.bfloat16)
        query_grad = (
            jnp.einsum("hts,she->the", score_grad, key_rows, preferred_element_type=f32)
            * score_scale
        )
        key_grad = (
            jnp.einsum("hts,the->she", score_grad, queries, preferred_element_type=f32)
            * score_scale
        )
        value_grad = jnp.einsum(
            "hts,the->she", softmax_f.astype(jnp.bfloat16), context_grad, preferred_element_type=f32
        )
        qkv_grad = (
            jnp.stack([query_grad, key_grad, value_grad], axis=1)
            .astype(jnp.bfloat16)
            .reshape(row_count, 3, local_width)
        )
        qkv_w_grad = jnp.einsum("td,tcn->dcn", normed, qkv_grad, preferred_element_type=f32)
        qv_bias_grad = jnp.sum(qkv_grad[:, 0::2].astype(f32), axis=0)
        normed_grad = input_total(
            jnp.einsum("tcn,dcn->td", qkv_grad, w_qkv[layer_idx], preferred_element_type=f32)
        )
        enter_grad, gain_attn, shift_attn = norm_back(
            entering, norm_gains[layer_idx, 0], norm_biases[layer_idx, 0], normed_grad
        )
        grad_rows = grad_rows + enter_grad
        small_parts.append(
            (
                jnp.stack([gain_attn, gain_mlp]),
                jnp.stack([shift_attn, shift_mlp]),
                jnp.stack([out_bias_grad, down_bias_grad]),
                qv_bias_grad,
                up_bias_grad,
            )
        )
        heavy = (qkv_w_grad, out_w_grad, up_w_grad, down_w_grad)
        heavy_parts.append(heavy)
    small_parts = small_parts[::-1]
    heavy_parts = heavy_parts[::-1]
    gain_grads = jnp.stack([entry[0] for entry in small_parts])
    shift_grads = jnp.stack([entry[1] for entry in small_parts])
    bias_grads = jnp.stack([entry[2] for entry in small_parts])
    qv_grads = jnp.stack([entry[3] for entry in small_parts])
    up_bias_grads = jnp.stack([entry[4] for entry in small_parts])
    gain_grads, shift_grads, bias_grads = (gain_grads, shift_grads, bias_grads)
    gain_grads, shift_grads, bias_grads, qv_grads, up_bias_grads = (
        lax.psum(gain_grads.astype(jnp.bfloat16), "dp").astype(jnp.float32),
        lax.psum(shift_grads.astype(jnp.bfloat16), "dp").astype(jnp.float32),
        lax.psum(bias_grads.astype(jnp.bfloat16), "dp").astype(jnp.float32),
        lax.psum(qv_grads.astype(jnp.bfloat16), "dp").astype(jnp.float32),
        lax.psum(up_bias_grads.astype(jnp.bfloat16), "dp").astype(jnp.float32),
    )
    qkv_all = jnp.stack([entry[0] for entry in heavy_parts])
    out_all = jnp.stack([entry[1] for entry in heavy_parts])
    up_all = jnp.stack([entry[2] for entry in heavy_parts])
    down_all = jnp.stack([entry[3] for entry in heavy_parts])
    qkv_all, out_all, up_all, down_all = (
        lax.psum_scatter(
            qkv_all.astype(jnp.bfloat16), "dp", scatter_dimension=1, tiled=True
        ).astype(jnp.float32),
        lax.psum_scatter(
            out_all.astype(jnp.bfloat16), "dp", scatter_dimension=2, tiled=True
        ).astype(jnp.float32),
        lax.psum_scatter(up_all.astype(jnp.bfloat16), "dp", scatter_dimension=1, tiled=True).astype(
            jnp.float32
        ),
        lax.psum_scatter(
            down_all.astype(jnp.bfloat16), "dp", scatter_dimension=2, tiled=True
        ).astype(jnp.float32),
    )
    return (
        block_rows,
        grad_rows,
        gain_grads,
        shift_grads,
        qkv_all,
        qv_grads,
        out_all,
        bias_grads,
        up_all,
        up_bias_grads,
        down_all,
    )


def solution(mesh):
    in_specs = (
        P("dp", None),
        P("dp", None),
        P("dp", None),
        P(),
        P(),
        P(None, None, None, "tensor"),
        P(None, None, "tensor"),
        P(None, "tensor", None),
        P(),
        P(None, None, "tensor"),
        P(None, "tensor"),
        P(None, "tensor", None),
    )
    out_specs = (
        P("dp", None),
        P("dp", None),
        P(),
        P(),
        P(None, "dp", None, "tensor"),
        P(None, None, "tensor"),
        P(None, "tensor", "dp"),
        P(),
        P(None, "dp", "tensor"),
        P(None, "tensor"),
        P(None, "tensor", "dp"),
    )
    return jax.shard_map(
        on_device, mesh=mesh, in_specs=in_specs, out_specs=out_specs, check_vma=False
    )
```

profile of v0, /device:TPU:0, one launch (start us, length us, event | category | flops | bytes accessed | tf_op | source)
XLA Modules:
  0.0 713.0 jit_solution(7808958398125200820)
XLA Ops:
  10.5 2.6 fusion.72
  15.1 2.7 fusion.153
  19.9 3.0 convolution_convert_fusion.11
  24.6 54.7 %all-reduce.10.cloned.1.call-done = bf16[512,1024]{1,0:T(8,128)(2,1)} async-done(((bf16[512,1024]{1,0:T(8,128)(2,1)}), bf16[512,1024]{1,0:T(8,128)(2,1)}) %all-reduce.10.cloned.1.call-update) | async-done | bytes 1048592 | tf_op jit(solution)/shard_map/psum | solution.py:69
  81.6 3.1 fusion.54
  86.1 2.5 fusion.77
  89.1 51.0 %all-reduce.12.cloned.1.call-done = bf16[512,1024]{1,0:T(8,128)(2,1)} async-done(((bf16[512,1024]{1,0:T(8,128)(2,1)}), bf16[512,1024]{1,0:T(8,128)(2,1)}) %all-reduce.12.cloned.1.call-update) | async-done | bytes 1048592 | tf_op jit(solution)/shard_map/psum | solution.py:69
  153.1 50.0 %all-reduce.14.cloned.1.call-done = bf16[512,1024]{1,0:T(8,128)(2,1)} async-done(((bf16[512,1024]{1,0:T(8,128)(2,1)}), bf16[512,1024]{1,0:T(8,128)(2,1)}) %all-reduce.14.cloned.1.call-update) | async-done | bytes 1048592 | tf_op jit(solution)/shard_map/psum | solution.py:69
  209.3 3.4 fusion.155
  216.5 50.8 %all-reduce.16.cloned.1.call-done = bf16[512,1024]{1,0:T(8,128)(2,1)} async-done(((bf16[512,1024]{1,0:T(8,128)(2,1)}), bf16[512,1024]{1,0:T(8,128)(2,1)}) %all-reduce.16.cloned.1.call-update) | async-done | bytes 1048592 | tf_op jit(solution)/shard_map/psum | solution.py:72
  285.5 3.6 bitcast_convert_fusion.1
  289.4 51.1 %all-reduce.18.cloned.1.call-done = bf16[512,1024]{1,0:T(8,128)(2,1)} async-done(((bf16[512,1024]{1,0:T(8,128)(2,1)}), bf16[512,1024]{1,0:T(8,128)(2,1)}) %all-reduce.18.cloned.1.call-update) | async-done | bytes 1048592 | tf_op jit(solution)/shard_map/psum | solution.py:72
  340.5 2.5 fusion.19
  348.3 3.6 fusion.156
  355.3 4.8 fusion.83
  361.4 45.2 %all-reduce.20.cloned.1.call-done = bf16[512,1024]{1,0:T(8,128)(2,1)} async-done(((bf16[512,1024]{1,0:T(8,128)(2,1)}), bf16[512,1024]{1,0:T(8,128)(2,1)}) %all-reduce.20.cloned.1.call-update) | async-done | bytes 1048592 | tf_op jit(solution)/shard_map/psum | solution.py:72
  415.7 3.7 copy.97
  422.1 3.6 multiply_reduce_fusion
  431.2 3.3 fusion.102
  436.3 3.7 convolution_convert_fusion.6
  441.7 3.6 bitcast_convert_fusion
  446.3 3.0 fusion.87
  452.9 3.8 convert_bitcast_fusion
  460.7 11.4 %copy.99 = bf16[2,1024,1024]{1,0,2:T(2,128)(2,1)} copy(bf16[2,1024,1024]{2,1,0:T(8,128)(2,1)} %pad_maximum_fusion.1) | data formatting | bytes 8388608
  472.1 5.6 copy.104
  477.8 2.8 convert_bitcast_fusion.2
  494.0 52.3 %all-reduce.22.cloned.1.call-done = (bf16[512,1024]{1,0:T(8,128)(2,1)}, bf16[512,1024]{1,0:T(8,128)(2,1)}) async-done(((bf16[512,1024]{1,0:T(8,128)(2,1)}, bf16[512,1024]{1,0:T(8,128)(2,1)}), (bf16[512,1024]{1,0:T(8,128)(2,1)}, bf16[512,1024]{1,0:T(8,128)(2,1)})) %all-reduce.22.cloned.1.call-update) | async-done | bytes 2097168 | tf_op jit(solution)/shard_map/psum | solution.py:69
  551.0 24.5 %all-reduce = (bf16[2,2,1024]{2,1,0:T(2,128)(2,1)S(1)}, bf16[2,2,1024]{2,1,0:T(2,128)(2,1)S(1)}, bf16[2,2,256]{2,1,0:T(2,128)(2,1)S(1)}, bf16[2,2,1024]{2,1,0:T(2,128)(2,1)S(1)}, bf16[2,1024]{1,0:T(2,128)(2,1)S(1)}) all-reduce(bf16[2,2,1024]{2,1,0:T(2,128)(2,1)S(1)} %pad_maximum_fusion.6, ...), channel_id=1, replica_groups=mesh['dp'=8,'tensor'=4] {'dp'}, use_global_device_ids=true, to_apply=%region_36.37 | all-reduce | flops 15360 | bytes 61440 | tf_op jit(solution)/shard_map/psum | solution.py:219
  578.5 4.6 add_add_fusion.4
  583.2 11.8 %reduce-scatter.9.cloned.1.call-done = bf16[2,128,3,256]{3,1,2,0:T(8,128)(2,1)} async-done(((bf16[2,1024,3,256]{3,1,2,0:T(8,128)(2,1)}), bf16[2,128,3,256]{3,1,2,0:T(8,128)(2,1)}) %reduce-scatter.9.cloned.1.call-update) | async-done | bytes 393232 | tf_op jit(solution)/shard_map/reduce_scatter | solution.py:230
  596.9 52.4 %reduce-scatter.15.cloned.1.call-done = bf16[128,2048]{1,0:T(8,128)(2,1)} async-done(((bf16[1024,2048]{1,0:T(8,128)(2,1)}), bf16[128,2048]{1,0:T(8,128)(2,1)}) %reduce-scatter.15.cloned.1.call-update) | async-done | bytes 524304
  652.3 51.5 %reduce-scatter.11.cloned.1.call-done = bf16[2,128,1024]{2,1,0:T(8,128)(2,1)} async-done(((bf16[2,1024,1024]{2,1,0:T(8,128)(2,1)}), bf16[2,128,1024]{2,1,0:T(8,128)(2,1)}) %reduce-scatter.11.cloned.1.call-update) | async-done | bytes 524304 | tf_op jit(solution)/shard_map/reduce_scatter | solution.py:236
  (299 shorter events, 121.2 us)
Async XLA Ops:
  7.2 3.3 copy-start
  7.2 3.2 copy-start.50
  7.2 3.3 copy-start.51
  7.2 72.1 %all-reduce.10.cloned.1.call-start = ((), (), s32[]{:S(2)}) async-start(), calls=%async_computation.4 | async-start | bytes 2097152 | tf_op jit(solution)/shard_map/psum | solution.py:69
  13.2 4.7 copy-start.31
  13.2 6.7 copy-start.22
  13.3 4.6 copy-start.35
  24.5 115.5 %all-reduce.12.cloned.1.call-start = ((), (), s32[]{:S(2)}) async-start(), calls=%async_computation.5 | async-start | bytes 2097152 | tf_op jit(solution)/shard_map/psum | solution.py:69
  81.6 4.5 copy-start.59
  88.6 114.5 %all-reduce.14.cloned.1.call-start = ((), (), s32[]{:S(2)}) async-start(), calls=%async_computation.6 | async-start | bytes 2097152 | tf_op jit(solution)/shard_map/psum | solution.py:69
  144.1 3.8 copy-start.23
  149.9 53.2 %copy-start.29 = (bf16[4,64,512]{2,1,0:T(8,128)(2,1)}, bf16[4,64,512]{2,1,0:T(8,128)(2,1)S(1)}, u32[]{:S(2)}) copy-start(bf16[4,64,512]{2,1,0:T(8,128)(2,1)S(1)} %convolution_convert_fusion.10) | copy-start | bytes 786436
  151.9 115.5 %all-reduce.16.cloned.1.call-start = ((), (), s32[]{:S(2)}) async-start(), calls=%async_computation.7 | async-start | bytes 2097152 | tf_op jit(solution)/shard_map/psum | solution.py:72
  203.2 3.1 copy-start.57
  207.6 5.1 copy-start.68
  216.0 124.5 %all-reduce.18.cloned.1.call-start = ((), (), s32[]{:S(2)}) async-start(), calls=%async_computation.8 | async-start | bytes 2097152 | tf_op jit(solution)/shard_map/psum | solution.py:72
  270.3 3.3 copy-start.4
  289.2 117.4 %all-reduce.20.cloned.1.call-start = ((), (), s32[]{:S(2)}) async-start(), calls=%async_computation.9 | async-start | bytes 2097152 | tf_op jit(solution)/shard_map/psum | solution.py:72
  344.7 3.6 copy-start.65
  345.5 6.5 copy-start.19
  348.3 4.6 copy-start.58
  355.2 137.0 %reduce-scatter.13.cloned.1.call-start = ((), (), s32[]{:S(2)}) async-start(), calls=%async_computation.12 | async-start | bytes 1179648
  355.3 4.9 copy-start.12
  355.3 4.9 copy-start.30
  421.8 124.6 %all-reduce.22.cloned.1.call-start = ((), (), s32[]{:S(2)}) async-start(), calls=%async_computation.14 | async-start | bytes 4194304 | tf_op jit(solution)/shard_map/psum | solution.py:69
  422.1 3.6 copy-start.2
  445.3 149.6 %reduce-scatter.9.cloned.1.call-start = ((), (), s32[]{:S(2)}) async-start(), calls=%async_computation.10 | async-start | bytes 3538944 | tf_op jit(solution)/shard_map/reduce_scatter | solution.py:230
  452.6 196.7 %reduce-scatter.15.cloned.1.call-start = ((), (), s32[]{:S(2)}) async-start(), calls=%async_computation.13 | async-start | bytes 4718592
  452.9 3.9 copy-start.21
  452.9 3.9 copy-start.66
  477.7 226.1 %reduce-scatter.11.cloned.1.call-start = ((), (), s32[]{:S(2)}) async-start(), calls=%async_computation.11 | async-start | bytes 4718592 | tf_op jit(solution)/shard_map/reduce_scatter | solution.py:236
  484.6 3.4 copy-start.56
  (50 other events, 99.7 us)
Sparse Core Ops, SparseCore 0:
  24.6 54.6 all-reduce.9
  88.7 51.2 all-reduce.11
  152.0 51.1 all-reduce.13
  216.1 51.1 all-reduce.15
  289.3 51.1 all-reduce.17
  355.3 51.1 all-reduce.19
  421.9 35.2 reduce-scatter.12
  460.2 86.1 all-reduce.21
  549.8 45.1 reduce-scatter.8
  598.1 51.1 reduce-scatter.14
  652.7 51.1 reduce-scatter.10
where the time goes:
time: 721 us; the launch traced here: 713 us
  waiting for transfers between devices  471 us (65%)
  matrix products  78.9 us (11%)
  other arithmetic  62.7 us (9%)
  local copies, waits for them, and re-layouts  58.7 us (8%)
  blocking collectives  24.5 us (3%)
  between operations  15.4 us (2%)
    psum x4, waiting for transfers between devices, branch_total(): lax.psum(partial_value.astype(jnp.bfloat16), 'tensor').astype(jnp.float32)  208 us
    psum x3, waiting for transfers between devices, input_total(): lax.psum(partial_value.astype(jnp.bfloat16), 'tensor').astype(jnp.float32)  147 us
    unnamed x13, waiting for transfers between devices  52.6 us
    reduce_scatter x1, waiting for transfers between devices, on_device(): lax.psum_scatter(up_all.astype(jnp.bfloat16), 'dp', scatter_dimension=1,...  51.5 us
    unnamed x150, local copies, waits for them, and re-layouts  47.4 us
    psum x1, blocking collectives, on_device(): lax.psum(gain_grads.astype(jnp.bfloat16), 'dp').astype(jnp.float32)  24.5 us
    reduce_sum x12, other arithmetic, layer_norm(): return centered * lax.rsqrt(variance + NORM_EPS) * gain_vec + shift_vec  19.1 us
  transfers between devices with their start and end apart: 11, of which 10 were waited for; matrix products, arithmetic and copies ran while one was open for 13% of the time, Pallas kernels for 0%

commit v1 on v0

--- a/solution.py
+++ b/solution.py
@@ -1,6 +1,10 @@
+import functools
+
 import jax
 import jax.numpy as jnp
 from jax import lax
+from jax.experimental import pallas as pl
+from jax.experimental.pallas import tpu as pltpu
 from jax.sharding import PartitionSpec as P
 
 HEADS = 16
@@ -40,7 +44,173 @@
     return (same_seq, row_gap, live_rows)
 
 
+MESH = pl.DeviceIdType.MESH
+LAG = 3
+
+
+def line_sum_kernel(n, p_ref, out_ref, rin, up, rx, up_send, in_recv, x_recv, out_send, out_recv):
+    chunks = p_ref.shape[0]
+    half = n // 2
+    me = lax.axis_index("tensor")
+    side = me // half
+    step = 1 - 2 * side
+    inward = me + step
+    outward = me - step
+    depth = side * (n - 1) + me * step
+
+    barrier = pltpu.get_barrier_semaphore()
+    pl.semaphore_signal(barrier, inc=1, device_id={"tensor": inward}, device_id_type=MESH)
+
+    @pl.when(depth > 0)
+    def _():
+        pl.semaphore_signal(barrier, inc=1, device_id={"tensor": outward}, device_id_type=MESH)
+        pl.semaphore_wait(barrier, 2)
+
+    @pl.when(depth == 0)
+    def _():
+        pl.semaphore_wait(barrier, 1)
+
+    def copy(source, target, send, recv, c, device):
+        return pltpu.make_async_remote_copy(
+            src_ref=source.at[c],
+            dst_ref=target.at[c],
+            send_sem=send.at[c],
+            recv_sem=recv.at[c],
+            device_id={"tensor": device},
+            device_id_type=MESH,
+        )
+
+    def loop(body, start=0, stop=chunks):
+        lax.fori_loop(start, stop, lambda c, carry: (body(c), carry)[1], 0)
+
+    f32 = jnp.float32
+
+    for role in range(half):
+        depth_zero = role == 0
+        middle = role == half - 1
+        target, target_sem = (rx, x_recv) if middle else (rin, in_recv)
+        source = p_ref if depth_zero else up
+
+        def rise(c, depth_zero=depth_zero, source=source, target=target, target_sem=target_sem):
+            if not depth_zero:
+                copy(rin, rin, up_send, in_recv, c, outward).wait_recv()
+                up[c] = (p_ref[c].astype(f32) + rin[c].astype(f32)).astype(up.dtype)
+            copy(source, target, up_send, target_sem, c, inward).start()
+
+        def fall(c, depth_zero=depth_zero, middle=middle, source=source):
+            if middle:
+                copy(rx, rx, up_send, x_recv, c, inward).wait_recv()
+                out_ref[c] = (source[c].astype(f32) + rx[c].astype(f32)).astype(out_ref.dtype)
+            else:
+                copy(out_ref, out_ref, out_send, out_recv, c, inward).wait_recv()
+            if not depth_zero:
+                copy(out_ref, out_ref, out_send, out_recv, c, outward).start()
+
+        def drain(c, depth_zero=depth_zero, source=source, target=target, target_sem=target_sem):
+            copy(source, target, up_send, target_sem, c, inward).wait_send()
+            if not depth_zero:
+                copy(out_ref, out_ref, out_send, out_recv, c, outward).wait_send()
+
+        @pl.when(depth == role)
+        def _(middle=middle, rise=rise, fall=fall, drain=drain):
+            if middle:
+                loop(rise, 0, LAG)
+
+                def both(c):
+                    rise(c)
+                    fall(c - LAG)
+
+                loop(both, LAG, chunks)
+                loop(fall, chunks - LAG, chunks)
+            else:
+                loop(rise)
+                loop(fall)
+            loop(drain)
+
+
+def line_sum(partial, n):
+    rows, width = partial.shape
+    chunks = 16
+    shape = (chunks, rows // chunks, width)
+    scratch = pltpu.VMEM(shape, partial.dtype)
+    sems = pltpu.SemaphoreType.DMA((chunks,))
+    out = pl.pallas_call(
+        functools.partial(line_sum_kernel, n),
+        out_shape=jax.ShapeDtypeStruct(shape, partial.dtype),
+        in_specs=[pl.BlockSpec(memory_space=pltpu.VMEM)],
+        out_specs=pl.BlockSpec(memory_space=pltpu.VMEM),
+        scratch_shapes=[scratch, scratch, scratch, sems, sems, sems, sems, sems],
+        compiler_params=pltpu.CompilerParams(
+            collective_id=0, has_side_effects=True, vmem_limit_bytes=12 << 20
+        ),
+        cost_estimate=pl.CostEstimate(
+            flops=30 * 10**9, bytes_accessed=2 * rows * width * 2, transcendentals=0
+        ),
+        name="line_sum",
+    )(partial.reshape(shape))
+    return out.reshape(rows, width)
+
+
+def small_sum_kernel(n, v_ref, out_ref, slots, send, recv):
+    me = lax.axis_index("dp")
+    barrier = pltpu.get_barrier_semaphore()
+    for k in range(1, n):
+        pl.semaphore_signal(
+            barrier, inc=1, device_id={"dp": lax.rem(me + k, n)}, device_id_type=MESH
+        )
+    pl.semaphore_wait(barrier, n - 1)
+    copies = []
+    for k in range(1, n):
+        copies.append(
+            pltpu.make_async_remote_copy(
+                src_ref=v_ref,
+                dst_ref=slots.at[me],
+                send_sem=send.at[k],
+                recv_sem=recv.at[k],
+                device_id={"dp": lax.rem(me + k, n)},
+                device_id_type=MESH,
+            )
+        )
+        copies[-1].start()
+    slots[me] = v_ref[...]
+    for k in range(1, n):
+        pltpu.make_async_remote_copy(
+            src_ref=v_ref,
+            dst_ref=slots.at[lax.rem(me + n - k, n)],
+            send_sem=send.at[k],
+            recv_sem=recv.at[k],
+            device_id={"dp": lax.rem(me + k, n)},
+            device_id_type=MESH,
+        ).wait_recv()
+    total = slots[0].astype(jnp.float32)
+    for k in range(1, n):
+        total = total + slots[k].astype(jnp.float32)
+    out_ref[...] = total
+    for one in copies:
+        one.wait_send()
+
+
+def small_sum(values, n):
+    return pl.pallas_call(
+        functools.partial(small_sum_kernel, n),
+        out_shape=jax.ShapeDtypeStruct(values.shape, jnp.float32),
+        in_specs=[pl.BlockSpec(memory_space=pltpu.VMEM)],
+        out_specs=pl.BlockSpec(memory_space=pltpu.VMEM),
+        scratch_shapes=[
+            pltpu.VMEM((n,) + values.shape, values.dtype),
+            pltpu.SemaphoreType.DMA((n,)),
+            pltpu.SemaphoreType.DMA((n,)),
+        ],
+        compiler_params=pltpu.CompilerParams(
+            collective_id=1, has_side_effects=True, vmem_limit_bytes=8 << 20
+        ),
+        name="small_sum",
+    )(values)
+
+
 def on_device(
+    n_dp,
+    n_tensor,
     block_input,
     cotangent,
     seq_lengths,
@@ -66,10 +236,14 @@
     slopes = jnp.exp2(-8.0 * head_index.astype(f32) / HEADS)
 
     def branch_total(partial_value):
-        return lax.psum(partial_value.astype(jnp.bfloat16), "tensor").astype(jnp.float32)
+        return line_sum(partial_value.astype(jnp.bfloat16), n_tensor).astype(jnp.float32)
 
     def input_total(partial_value):
-        return lax.psum(partial_value.astype(jnp.bfloat16), "tensor").astype(jnp.float32)
+        return line_sum(partial_value.astype(jnp.bfloat16), n_tensor).astype(jnp.float32)
+
+    def dp_share(*grads):
+        joined = jnp.concatenate([grad.astype(jnp.bfloat16) for grad in grads], axis=1)
+        return lax.psum_scatter(joined, "dp", scatter_dimension=0, tiled=True)
 
     def score_block(queries, key_rows):
         raw_scores = (
@@ -79,6 +253,7 @@
         return jnp.where(same_seq, raw_scores, -1000000000.0)
 
     head_shape = (row_count, heads_here, HEAD_DIM)
+    w_rows = w_qkv.transpose(0, 2, 1, 3)
     residual = block_input.astype(f32)
     stored = []
     for layer_idx in range(depth):
@@ -86,11 +261,11 @@
         normed = layer_norm(residual, norm_gains[layer_idx, 0], norm_biases[layer_idx, 0]).astype(
             jnp.bfloat16
         )
-        projected = jnp.einsum("td,dcn->tcn", normed, w_qkv[layer_idx], preferred_element_type=f32)
-        queries = (projected[:, 0] + qv_bias[layer_idx, 0]).astype(jnp.bfloat16).reshape(head_shape)
-        key_rows = projected[:, 1].astype(jnp.bfloat16).reshape(head_shape)
+        projected = jnp.einsum("td,cdn->ctn", normed, w_rows[layer_idx], preferred_element_type=f32)
+        queries = (projected[0] + qv_bias[layer_idx, 0]).astype(jnp.bfloat16).reshape(head_shape)
+        key_rows = projected[1].astype(jnp.bfloat16).reshape(head_shape)
         value_rows = (
-            (projected[:, 2] + qv_bias[layer_idx, 1]).astype(jnp.bfloat16).reshape(head_shape)
+            (projected[2] + qv_bias[layer_idx, 1]).astype(jnp.bfloat16).reshape(head_shape)
         )
         scores = score_block(queries, key_rows)
         row_max = jnp.max(scores, axis=-1, keepdims=True)
@@ -109,7 +284,11 @@
         )
         activated = gelu_tanh(up_proj).astype(jnp.bfloat16)
         partial_value = jnp.dot(activated, w_down[layer_idx], preferred_element_type=f32)
-        residual = residual + branch_total(partial_value) + out_biases[layer_idx, 1]
+        if layer_idx == depth - 1:
+            total = lax.psum(partial_value.astype(jnp.bfloat16), "tensor").astype(f32)
+        else:
+            total = branch_total(partial_value)
+        residual = residual + total + out_biases[layer_idx, 1]
         stored.append(
             (
                 entering,
@@ -145,11 +324,12 @@
         ) = stored[layer_idx]
         down_bias_grad = jnp.sum(grad_rows, axis=0)
         grad_low = grad_rows.astype(jnp.bfloat16)
-        down_w_grad = jnp.einsum("tf,td->fd", activated, grad_low, preferred_element_type=f32)
+        down_w_grad = jnp.einsum("td,tf->df", grad_low, activated, preferred_element_type=f32)
         act_grad = jnp.einsum("td,fd->tf", grad_low, w_down[layer_idx], preferred_element_type=f32)
         up_grad = jax.vjp(gelu_tanh, up_proj)[1](act_grad)[0].astype(jnp.bfloat16)
         up_bias_grad = jnp.sum(up_grad.astype(f32), axis=0)
         up_w_grad = jnp.einsum("td,tf->df", normed_mlp, up_grad, preferred_element_type=f32)
+        mlp_sum = dp_share(up_w_grad, down_w_grad)
         normed_grad = input_total(
             jnp.einsum("tf,df->td", up_grad, w_up[layer_idx], preferred_element_type=f32)
         )
@@ -159,7 +339,7 @@
         grad_rows = grad_rows + middle_grad
         out_bias_grad = jnp.sum(grad_rows, axis=0)
         grad_low = grad_rows.astype(jnp.bfloat16)
-        out_w_grad = jnp.einsum("tn,td->nd", context, grad_low, preferred_element_type=f32)
+        out_w_grad = jnp.einsum("td,tn->dn", grad_low, context, preferred_element_type=f32)
         context_grad = jnp.einsum(
             "td,nd->tn", grad_low, w_out[layer_idx], preferred_element_type=f32
         )
@@ -182,15 +362,23 @@
         value_grad = jnp.einsum(
             "hts,the->she", softmax_f.astype(jnp.bfloat16), context_grad, preferred_element_type=f32
         )
-        qkv_grad = (
-            jnp.stack([query_grad, key_grad, value_grad], axis=1)
-            .astype(jnp.bfloat16)
-            .reshape(row_count, 3, local_width)
-        )
-        qkv_w_grad = jnp.einsum("td,tcn->dcn", normed, qkv_grad, preferred_element_type=f32)
-        qv_bias_grad = jnp.sum(qkv_grad[:, 0::2].astype(f32), axis=0)
+        query_grad, key_grad, value_grad = (
+            grad.astype(jnp.bfloat16).reshape(row_count, local_width)
+            for grad in (query_grad, key_grad, value_grad)
+        )
+        attn_sum = dp_share(
+            *(
+                jnp.einsum("td,tn->dn", normed, grad, preferred_element_type=f32)
+                for grad in (query_grad, key_grad, value_grad)
+            ),
+            out_w_grad,
+        )
+        qv_bias_grad = jnp.stack(
+            [jnp.sum(query_grad.astype(f32), axis=0), jnp.sum(value_grad.astype(f32), axis=0)]
+        )
+        qkv_grad = jnp.stack([query_grad, key_grad, value_grad])
         normed_grad = input_total(
-            jnp.einsum("tcn,dcn->td", qkv_grad, w_qkv[layer_idx], preferred_element_type=f32)
+            jnp.einsum("ctn,cdn->td", qkv_grad, w_rows[layer_idx], preferred_element_type=f32)
         )
         enter_grad, gain_attn, shift_attn = norm_back(
             entering, norm_gains[layer_idx, 0], norm_biases[layer_idx, 0], normed_grad
@@ -205,7 +393,14 @@
                 up_bias_grad,
             )
         )
-        heavy = (qkv_w_grad, out_w_grad, up_w_grad, down_w_grad)
+        width = 3 * local_width
+        hidden = w_up.shape[2]
+        heavy = (
+            attn_sum[:, :width].astype(f32).reshape(-1, 3, local_width),
+            attn_sum[:, width:].astype(f32).T,
+            mlp_sum[:, :hidden].astype(f32),
+            mlp_sum[:, hidden:].astype(f32).T,
+        )
         heavy_parts.append(heavy)
     small_parts = small_parts[::-1]
     heavy_parts = heavy_parts[::-1]
@@ -214,32 +409,21 @@
     bias_grads = jnp.stack([entry[2] for entry in small_parts])
     qv_grads = jnp.stack([entry[3] for entry in small_parts])
     up_bias_grads = jnp.stack([entry[4] for entry in small_parts])
-    gain_grads, shift_grads, bias_grads = (gain_grads, shift_grads, bias_grads)
-    gain_grads, shift_grads, bias_grads, qv_grads, up_bias_grads = (
-        lax.psum(gain_grads.astype(jnp.bfloat16), "dp").astype(jnp.float32),
-        lax.psum(shift_grads.astype(jnp.bfloat16), "dp").astype(jnp.float32),
-        lax.psum(bias_grads.astype(jnp.bfloat16), "dp").astype(jnp.float32),
-        lax.psum(qv_grads.astype(jnp.bfloat16), "dp").astype(jnp.float32),
-        lax.psum(up_bias_grads.astype(jnp.bfloat16), "dp").astype(jnp.float32),
-    )
+    pieces = (gain_grads, shift_grads, bias_grads, qv_grads, up_bias_grads)
+    flat = jnp.concatenate([piece.reshape(-1) for piece in pieces])
+    unit = 16 * 1024
+    flat = jnp.pad(flat, (0, -flat.size % unit)).astype(jnp.bfloat16).reshape(-1, 1024)
+    flat = small_sum(flat, n_dp).reshape(-1)
+    summed = []
+    offset = 0
+    for piece in pieces:
+        summed.append(flat[offset : offset + piece.size].reshape(piece.shape))
+        offset += piece.size
+    gain_grads, shift_grads, bias_grads, qv_grads, up_bias_grads = summed
     qkv_all = jnp.stack([entry[0] for entry in heavy_parts])
     out_all = jnp.stack([entry[1] for entry in heavy_parts])
     up_all = jnp.stack([entry[2] for entry in heavy_parts])
     down_all = jnp.stack([entry[3] for entry in heavy_parts])
-    qkv_all, out_all, up_all, down_all = (
-        lax.psum_scatter(
-            qkv_all.astype(jnp.bfloat16), "dp", scatter_dimension=1, tiled=True
-        ).astype(jnp.float32),
-        lax.psum_scatter(
-            out_all.astype(jnp.bfloat16), "dp", scatter_dimension=2, tiled=True
-        ).astype(jnp.float32),
-        lax.psum_scatter(up_all.astype(jnp.bfloat16), "dp", scatter_dimension=1, tiled=True).astype(
-            jnp.float32
-        ),
-        lax.psum_scatter(
-            down_all.astype(jnp.bfloat16), "dp", scatter_dimension=2, tiled=True
-        ).astype(jnp.float32),
-    )
     return (
         block_rows,
         grad_rows,
@@ -284,5 +468,5 @@
         P(None, "tensor", "dp"),
     )
     return jax.shard_map(
-        on_device, mesh=mesh, in_specs=in_specs, out_specs=out_specs, check_vma=False
+        functools.partial(on_device, mesh.shape["dp"], mesh.shape["tensor"]), mesh=mesh, in_specs=in_specs, out_specs=out_specs, check_vma=False
     )

time: 721 us -> 513 us (0.71)
  waiting for transfers between devices: 471 us -> 60.9 us
  Pallas kernels: 0 us -> 264 us
  blocking collectives: 24.5 us -> 0 us
  other arithmetic: 62.7 us -> 39.1 us
  matrix products: 78.9 us -> 59.3 us
    psum x7 -> x1, waiting for transfers between devices: 355 us -> 0.02 us  [on_device(): total = lax.psum(partial_value.astype(jnp.bfloat16), 'tensor').astype(f32)]
    pallas_call x0 -> x8, Pallas kernels: none -> 264 us  [the longest x7 254 us: line_sum(): pl.pallas_call(functools.partial(line_sum_kernel, n), out_shape=jax.Shape...]
    reduce_scatter x2 -> x0, waiting for transfers between devices: 63.3 us -> none  [the longest x1 51.5 us: on_device(): lax.psum_scatter(up_all.astype(jnp.bfloat16), 'dp', scatter_dimension=1,...]
    psum x1 -> x0, blocking collectives: 24.5 us -> none  [on_device(): lax.psum(gain_grads.astype(jnp.bfloat16), 'dp').astype(jnp.float32)]
    reduce_sum x12, other arithmetic: 19.1 us -> 7.27 us  [layer_norm(): return centered * lax.rsqrt(variance + NORM_EPS) * gain_vec + shift_vec]
    unnamed x13 -> x9, waiting for transfers between devices: 52.6 us -> 60.9 us
    convert_element_type x9 -> x2, other arithmetic: 8.86 us -> 0.85 us  [on_device(): layer_norm(residual, norm_gains[layer_idx, 0], norm_biases[layer_idx, 0])]
    concatenate x0 -> x4, other arithmetic: none -> 7.98 us  [dp_share(): jnp.concatenate([grad.astype(jnp.bfloat16) for grad in grads], axis=1)]
  transfers between devices with their start and end apart: 11 -> 5, of which waited for: 10 -> 2; matrix products, arithmetic and copies ran while one was open for 13% -> 16% of each run, Pallas kernels for 0% -> 26%
where the time goes in v1:
time: 513 us; the launch traced here: 504 us
  Pallas kernels  264 us (51%)
  local copies, waits for them, and re-layouts  64.5 us (13%)
  waiting for transfers between devices  60.9 us (12%)
  matrix products  59.3 us (12%)
  other arithmetic  39.1 us (8%)
  between operations  15.9 us (3%)
    pallas_call x7, Pallas kernels, line_sum(): pl.pallas_call(functools.partial(line_sum_kernel, n), out_shape=jax.Shape...  254 us
    unnamed x9, waiting for transfers between devices  60.9 us
    unnamed x216, local copies, waits for them, and re-layouts  50.7 us
    dot_general x2, matrix products, on_device(): jnp.einsum('td,fd->tf', grad_low, w_down[layer_idx], preferred_element_ty...  11.7 us
  transfers between devices with their start and end apart: 5, of which 2 were waited for; matrix products, arithmetic and copies ran while one was open for 16% of the time, Pallas kernels for 26%

profile of v1, /device:TPU:0, one launch (start us, length us, event | category | flops | bytes accessed | tf_op | source)
XLA Modules:
  0.0 504.0 jit_solution(9519160074146304388)
XLA Ops:
  7.4 1.9 convert_reduce_fusion
  10.5 4.7 copy.63
  15.6 2.8 convolution_bitcast_fusion.1
  25.6 35.6 %line_sum.7 = bf16[16,32,1024]{2,1,0:T(8,128)(2,1)S(1)} custom-call(bf16[16,32,1024]{2,1,0:T(8,128)(2,1)S(1)} %bitcast.276), custom_call_target="tpu_custom_call" | custom-call | flops 30000001024 | bytes 2097152 | tf_op jit(solution)/shard_map/line_sum/pallas_call | solution.py:137
  62.4 2.3 copy-done.86
  68.4 31.5 %line_sum.8 = bf16[16,32,1024]{2,1,0:T(8,128)(2,1)S(1)} custom-call(bf16[16,32,1024]{2,1,0:T(8,128)(2,1)S(1)} %bitcast.280), custom_call_target="tpu_custom_call" | custom-call | flops 30000001024 | bytes 2097152 | tf_op jit(solution)/shard_map/line_sum/pallas_call | solution.py:137
  105.5 2.9 fusion.154
  112.2 30.9 %line_sum.9 = bf16[16,32,1024]{2,1,0:T(8,128)(2,1)S(1)} custom-call(bf16[16,32,1024]{2,1,0:T(8,128)(2,1)S(1)} %bitcast.277), custom_call_target="tpu_custom_call" | custom-call | flops 30000001024 | bytes 2097152 | tf_op jit(solution)/shard_map/line_sum/pallas_call | solution.py:137
  143.8 2.1 copy-done.87
  148.7 2.5 fusion.79
  152.5 5.8 %fusion.155 = (bf16[1024]{0:T(1024)(128)(2,1)}, bf16[512,1024]{1,0:T(8,128)(2,1)S(1)}) fusion(bf16[2,1024,1024]{2,1,0:T(8,128)(2,1)} %param.23, bf16[512,1024]{1,0:T(8,128)(2,1)S(1)} %copy-done.41, f32[512]{0:T(512)S(1)} %fusion.126, f32[512,1024]{1,0:T(8,128)} %copy-done.93, f32[1024]{0:T(1024)S(1)} %bitcast.361), kind=kOutput, calls=%fused_computation.278 | convolution fusion | flops 1088945152 | bytes 6299648 | tf_op jit(solution)/shard_map/td,fd->tf/dot_general | solution.py:328
  159.6 61.3 %line_sum.10 = bf16[16,32,1024]{2,1,0:T(8,128)(2,1)S(1)} custom-call(bf16[16,32,1024]{2,1,0:T(8,128)(2,1)S(1)} %bitcast.281), custom_call_target="tpu_custom_call" | custom-call | flops 30000001024 | bytes 2097152 | tf_op jit(solution)/shard_map/line_sum/pallas_call | solution.py:137
  222.7 3.4 fusion.138
  236.0 2.5 bitcast_convert_fusion.1
  238.5 33.7 %line_sum.11 = bf16[16,32,1024]{2,1,0:T(8,128)(2,1)S(1)} custom-call(bf16[16,32,1024]{2,1,0:T(8,128)(2,1)S(1)} %bitcast.279), custom_call_target="tpu_custom_call" | custom-call | flops 30000001024 | bytes 2097152 | tf_op jit(solution)/shard_map/line_sum/pallas_call | solution.py:137
  274.3 2.1 fusion.137
  279.1 4.0 copy.95
  283.7 5.9 %fusion.156 = (bf16[1024]{0:T(1024)(128)(2,1)S(1)}, bf16[512,1024]{1,0:T(8,128)(2,1)S(1)}) fusion(bf16[2,1024,1024]{2,1,0:T(8,128)(2,1)} %param.23, f32[512,1024]{1,0:T(8,128)} %get-tuple-element.59, f32[512,1024]{1,0:T(8,128)} %copy-done.91, f32[1024]{0:T(1024)S(1)} %bitcast.358), kind=kOutput, calls=%fused_computation.279 | convolution fusion | flops 1087896576 | bytes 7346176 | tf_op jit(solution)/shard_map/td,fd->tf/dot_general | solution.py:328
  290.9 31.0 %line_sum.12 = bf16[16,32,1024]{2,1,0:T(8,128)(2,1)S(1)} custom-call(bf16[16,32,1024]{2,1,0:T(8,128)(2,1)S(1)} %bitcast.282), custom_call_target="tpu_custom_call" | custom-call | flops 30000001024 | bytes 2097152 | tf_op jit(solution)/shard_map/line_sum/pallas_call | solution.py:137
  336.1 3.9 copy.93
  340.7 3.5 convolution_convert_fusion.1
  345.9 2.4 pad_maximum_fusion.1
  348.3 6.6 %copy.99 = bf16[1024,2048]{1,0:T(8,128)(2,1)} copy(bf16[1024,2048]{0,1:T(8,128)(2,1)} %pad_maximum_fusion.1) | data formatting | bytes 8388608
  356.0 3.4 convolution_convert_fusion.3
  361.0 2.4 pad_maximum_fusion
  363.4 6.6 %copy.97 = bf16[1024,2048]{1,0:T(8,128)(2,1)} copy(bf16[1024,2048]{0,1:T(8,128)(2,1)} %pad_maximum_fusion) | data formatting | bytes 8388608
  370.7 3.4 bitcast_convert_fusion
  375.8 30.6 %line_sum.13 = bf16[16,32,1024]{2,1,0:T(8,128)(2,1)S(1)} custom-call(bf16[16,32,1024]{2,1,0:T(8,128)(2,1)S(1)} %bitcast.278), custom_call_target="tpu_custom_call" | custom-call | flops 30000001024 | bytes 2097152 | tf_op jit(solution)/shard_map/line_sum/pallas_call | solution.py:137
  408.8 9.2 %small_sum.1 = f32[16,1024]{1,0:T(8,128)S(1)} custom-call(bf16[16,1024]{1,0:T(8,128)(2,1)S(1)} %reshape.417.v_ref), custom_call_target="tpu_custom_call" | custom-call | tf_op jit(solution)/shard_map/small_sum/pallas_call | solution.py:194
  421.1 3.7 add_add_fusion.4
  431.0 7.8 %reduce-scatter.19.cloned.1.call-done = bf16[128,2048]{1,0:T(8,128)(2,1)} async-done(((bf16[1024,2048]{1,0:T(8,128)(2,1)}), bf16[128,2048]{1,0:T(8,128)(2,1)}) %reduce-scatter.19.cloned.1.call-update) | async-done | bytes 524304
  440.2 53.0 %reduce-scatter.17.cloned.1.call-done = bf16[128,2048]{1,0:T(8,128)(2,1)} async-done(((bf16[1024,2048]{1,0:T(8,128)(2,1)}), bf16[128,2048]{1,0:T(8,128)(2,1)}) %reduce-scatter.17.cloned.1.call-update) | async-done | bytes 524304
  (374 shorter events, 84.8 us)
Async XLA Ops:
  7.2 215.4 %all-reduce.3.cloned.1.call-start = ((), (), s32[]{:S(2)}) async-start(), calls=%async_computation.4 | async-start | bytes 2097152 | tf_op jit(solution)/shard_map/psum | solution.py:288
  7.4 13.1 %copy-start.47 = (f32[512,512]{0,1:T(8,128)}, f32[512,512]{0,1:T(8,128)S(1)}, u32[]{:S(2)}) copy-start(f32[512,512]{0,1:T(8,128)S(1)} %subtract_convert_fusion) | copy-start | bytes 3145732
  9.4 5.8 %copy-start.53 = (f32[512]{0:T(512)}, f32[512]{0:T(512)S(1)}, u32[]{:S(2)}) copy-start(f32[512]{0:T(512)S(1)} %broadcast_multiply_fusion.3) | copy-start | bytes 6148
  10.4 4.8 copy-start.57
  10.4 4.8 copy-start.51
  10.4 52.0 %copy-start.55 = (f32[1,1,1024]{2,1,0:T(1,128)}, f32[1,1,1024]{2,1,0:T(1,128)S(1)}, u32[]{:S(2)}) copy-start(f32[1,1,1024]{2,1,0:T(1,128)S(1)} %get-tuple-element.86) | copy-start | bytes 12292
  10.4 52.0 %copy-start.79 = (f32[1,1,1024]{2,1,0:T(1,128)}, f32[1,1,1024]{2,1,0:T(1,128)S(1)}, u32[]{:S(2)}) copy-start(f32[1,1,1024]{2,1,0:T(1,128)S(1)} %get-tuple-element.90) | copy-start | bytes 12292
  10.4 133.4 %copy-start.81 = (f32[1,1,1024]{2,1,0:T(1,128)}, f32[1,1,1024]{2,1,0:T(1,128)S(1)}, u32[]{:S(2)}) copy-start(f32[1,1,1024]{2,1,0:T(1,128)S(1)} %get-tuple-element.89) | copy-start | bytes 12292
  18.7 3.9 copy-start.22
  19.6 46.5 %copy-start.75 = (f32[1,1024]{1,0:T(1,128)}, f32[1,1024]{1,0:T(1,128)S(1)}, u32[]{:S(2)}) copy-start(f32[1,1024]{1,0:T(1,128)S(1)} %get-tuple-element.94) | copy-start | bytes 12292
  19.6 132.9 %copy-start.77 = (f32[1,1024]{1,0:T(1,128)}, f32[1,1024]{1,0:T(1,128)S(1)}, u32[]{:S(2)}) copy-start(f32[1,1024]{1,0:T(1,128)S(1)} %get-tuple-element.93) | copy-start | bytes 12292
  24.8 36.6 %copy-start.33 = (bf16[4,64,512]{2,1,0:T(8,128)(2,1)}, bf16[4,64,512]{2,1,0:T(8,128)(2,1)S(1)}, u32[]{:S(2)}) copy-start(bf16[4,64,512]{2,1,0:T(8,128)(2,1)S(1)} %convolution_convert_fusion.19) | copy-start | bytes 786436
  100.6 42.4 %copy-start.5 = (f32[512,1024]{1,0:T(8,128)}, f32[512,1024]{1,0:T(8,128)S(1)}, u32[]{:S(2)}) copy-start(f32[512,1024]{1,0:T(8,128)S(1)} %get-tuple-element.65) | copy-start | bytes 6291460
  103.2 132.0 %copy-start.18 = (bf16[512,1024]{1,0:T(8,128)(2,1)}, bf16[512,1024]{1,0:T(8,128)(2,1)S(1)}, u32[]{:S(2)}) copy-start(bf16[512,1024]{1,0:T(8,128)(2,1)S(1)} %add_convert_fusion.2) | copy-start | bytes 3145732
  104.3 4.1 copy-start.45
  151.2 273.6 %reduce-scatter.15.cloned.1.call-start = ((), (), s32[]{:S(2)}) async-start(), calls=%async_computation.6 | async-start | bytes 2359296
  152.5 5.8 %copy-start.88 = (bf16[2,1024,1024]{2,1,0:T(8,128)(2,1)S(1)}, bf16[2,1024,1024]{2,1,0:T(8,128)(2,1)}, u32[]{:S(2)}) copy-start(bf16[2,1024,1024]{2,1,0:T(8,128)(2,1)} %param.21) | copy-start | bytes 12582916
  159.6 61.3 %copy-start.10 = (f32[512,1024]{1,0:T(8,128)S(1)}, f32[512,1024]{1,0:T(8,128)}, u32[]{:S(2)}) copy-start(f32[512,1024]{1,0:T(8,128)} %copy-done.9) | copy-start | bytes 6291460
  238.5 33.7 %copy-start.6 = (f32[512,1024]{1,0:T(8,128)S(1)}, f32[512,1024]{1,0:T(8,128)}, u32[]{:S(2)}) copy-start(f32[512,1024]{1,0:T(8,128)} %copy-done.5) | copy-start | bytes 6291460
  283.0 144.0 %reduce-scatter.13.cloned.1.call-start = ((), (), s32[]{:S(2)}) async-start(), calls=%async_computation.5 | async-start | bytes 2359296
  283.7 5.9 %copy-start.89 = (bf16[2,1024,1024]{2,1,0:T(8,128)(2,1)S(1)}, bf16[2,1024,1024]{2,1,0:T(8,128)(2,1)}, u32[]{:S(2)}) copy-start(bf16[2,1024,1024]{2,1,0:T(8,128)(2,1)} %param.21) | copy-start | bytes 12582916
  290.9 31.0 %copy-start.12 = (f32[512,1024]{1,0:T(8,128)S(1)}, f32[512,1024]{1,0:T(8,128)}, u32[]{:S(2)}) copy-start(f32[512,1024]{1,0:T(8,128)} %copy-done.11) | copy-start | bytes 6291460
  290.9 31.0 %copy-start.56 = (f32[1,1,1024]{2,1,0:T(1,128)S(1)}, f32[1,1,1024]{2,1,0:T(1,128)}, u32[]{:S(2)}) copy-start(f32[1,1,1024]{2,1,0:T(1,128)} %copy-done.55) | copy-start | bytes 12292
  324.9 9.2 %copy-start.13 = (f32[512,1024]{1,0:T(8,128)}, f32[512,1024]{1,0:T(8,128)S(1)}, u32[]{:S(2)}) copy-start(f32[512,1024]{1,0:T(8,128)S(1)} %get-tuple-element.57) | copy-start | bytes 6291460
  340.1 4.1 copy-start.78
  340.1 98.7 %reduce-scatter.19.cloned.1.call-start = ((), (), s32[]{:S(2)}) async-start(), calls=%async_computation.8 | async-start | bytes 4718592
  355.0 138.2 %reduce-scatter.17.cloned.1.call-start = ((), (), s32[]{:S(2)}) async-start(), calls=%async_computation.7 | async-start | bytes 4718592
  363.4 6.7 %copy-start.36 = (bf16[4,64,512]{2,1,0:T(8,128)(2,1)S(1)}, bf16[4,64,512]{2,1,0:T(8,128)(2,1)}, u32[]{:S(2)}) copy-start(bf16[4,64,512]{2,1,0:T(8,128)(2,1)} %copy-done.35) | copy-start | bytes 786436
  363.4 7.0 %copy-start.32 = (bf16[4,64,512]{2,1,0:T(8,128)(2,1)S(1)}, bf16[4,64,512]{2,1,0:T(8,128)(2,1)}, u32[]{:S(2)}) copy-start(bf16[4,64,512]{2,1,0:T(8,128)(2,1)} %copy-done.31) | copy-start | bytes 786436
  375.8 30.9 %copy-start.8 = (bf16[512,1024]{1,0:T(8,128)(2,1)S(1)}, bf16[512,1024]{1,0:T(8,128)(2,1)}, u32[]{:S(2)}) copy-start(bf16[512,1024]{1,0:T(8,128)(2,1)} %param.12) | copy-start | bytes 3145732
  375.8 30.9 %copy-start.52 = (f32[1,1,1024]{2,1,0:T(1,128)S(1)}, f32[1,1,1024]{2,1,0:T(1,128)}, u32[]{:S(2)}) copy-start(f32[1,1,1024]{2,1,0:T(1,128)} %copy-done.51) | copy-start | bytes 12292
  375.8 30.9 %copy-start.54 = (f32[512]{0:T(512)S(1)}, f32[512]{0:T(512)}, u32[]{:S(2)}) copy-start(f32[512]{0:T(512)} %copy-done.53) | copy-start | bytes 6148
  (70 other events, 137.2 us)
Sparse Core Ops, SparseCore 0:
  151.3 71.2 all-reduce.2
  283.2 41.0 reduce-scatter.14
  340.2 41.3 reduce-scatter.12
  384.8 53.9 reduce-scatter.18
  442.0 51.1 reduce-scatter.16
